TPU v7x, 128 devices: a whole 4x4x4 slice. The times are simulated.
128 devices in a mesh: gran: 32 (over x, z, core), band: 4 (over y).
Axes of the slice: x: 4, y: 4, z: 4, core: 2. Of those that a mesh axis runs over, the one named last changes fastest.
Arguments:
- prior_grids: float32 [512, 12, 2, 4096], P('gran', 'band'), may hold values from -1.5 to 1.5
- pif_rhs: float32 [512, 12, 2, 4096], P('gran', 'band'), may hold values from -8 to 8
- pif_diagonal: float32 [512, 12, 2, 4096], P('gran', 'band'), may hold values from 0.5 to 2
- pif_cross: float32 [512, 12, 4096], P('gran', 'band'), may hold values from -0.7 to 0.7
- pif_coupling: bfloat16 [512, 8, 12, 4096], P('gran', None, 'band'), may hold values from 0.25 to 2
- neighbour_offset: int32 [512, 8], P('gran'), may hold values from -4 to 4, as said below
- neighbour_count: int32 [512], P('gran'), may hold values from 1 to 8, as said below
- tile_route: int32 [512, 2], replicated, may hold values from 0 to 31, all different within a row; in each aligned block of 16 rows (0 to 15, 16 to 31, ...) at most 2 rows name the same one
- tile_window: int32 [512, 2, 2], replicated, may hold values from 0 to 1760
- tile_pixels: bfloat16 [32, 12, 256, 256], P('gran', 'band'), may hold values from 0.049804688 to 1
Outputs:
- balanced_grids: float32 [512, 12, 2, 4096], P('gran', 'band')
- corrected_tiles: bfloat16 [32, 12, 256, 256], P('gran', 'band')
Inputs may be any that keep to these rules, and one draw needn't show every extreme that they name: `neighbour_offset`: A granule's slots below its count hold a nonzero offset to another granule; the other slots hold 0. In every aligned block of 16 granules the granule of count 8 has an offset of magnitude 4 in its first slot. `neighbour_count`: every aligned block of 16 granules holds a granule with 8 neighbours. `tile_route`: each granule names two different tiles; every tile is named; among the 16 granules of one device no tile is named more than 2 times.
All inputs are finite; a program needn't handle non-finite values.
Results may differ from a plain program's by a relative error of at most 0.0036.
The roundings to bfloat16 on the way count: a program that leaves them out, or rounds other values in their place, can miss the bound.
Values may be sent and summed in bfloat16 or wider, within the bound.
A program may use at most 128 MiB of HBM per device.

v0:
```python
import jax
import jax.numpy as jnp
from jax import lax
from jax.experimental import pallas as pl
from jax.experimental.pallas import tpu as pltpu
from jax.sharding import PartitionSpec as P

MESH = pl.DeviceIdType.MESH
F32 = jnp.float32
BF16 = jnp.bfloat16
I32 = jnp.int32

BANDS = 12
PATCH = 8
REACH = 4
SWEEPS = 3
SP = 32
ROBUST = 0.3 * BANDS * PATCH * PATCH

GD = 16
BD_ = 3
NG = 32
NB = 4
SLOTS = 8
PIX = 256
WIN = 16
FIRST_MAX = 64 - WIN
FAR = 1000.0


def iota(shape, dim):
    return lax.broadcasted_iota(I32, shape, dim)


def dot(a, b):
    return jnp.dot(a, b, preferred_element_type=F32)


def split_dot(x, table):
    high = x.astype(BF16)
    low = (x - high.astype(F32)).astype(BF16)
    return dot(high, table) + dot(low, table)


def butterfly(x, lane, width, op):
    size = x.shape[1]
    step = 1
    while step < width:
        other = jnp.where(
            (lane // step) % 2 == 0,
            pltpu.roll(x, size - step, axis=1),
            pltpu.roll(x, step, axis=1),
        )
        x = op(x, other)
        step *= 2
    return x


def far_tap(d):
    return ((-0.5 * d + 2.5) * d - 4.0) * d + 2.0


def near_tap(d):
    return (1.5 * d - 2.5) * d * d + 1.0


def edge_granule(k):
    return k + (k // 4) * 8


def inner_granule(k):
    return k + 4


def kernel(
    off_s,
    cnt_s,
    prior_h,
    rhs_h,
    diag_h,
    cross_h,
    coup_h,
    route_v,
    win_v,
    pix_h,
    bal_h,
    tile_h,
    prior_b,
    rhs_b,
    diag_b,
    cross_b,
    coup_b,
    pix_b,
    out_b,
    tile_b,
    grids,
    resp,
    coup,
    cterm,
    disp,
    spread,
    weight,
    halo_out,
    halo_in,
    part_out,
    part_in,
    tab_v,
    tab_s,
    pay_out,
    pay_in,
    roww,
    colw,
    diagonal,
    rowpass,
    in_sem,
    out_sem,
    hs_sem,
    hr_sem,
    ps_sem,
    pr_sem,
    as_sem,
    ar_sem,
    tab_sem,
    own_sem,
):
    me = lax.axis_index("gran")
    mb = lax.axis_index("band")
    right = lax.rem(me + 1, NG)
    left = lax.rem(me + NG - 1, NG)

    loads = [
        pltpu.make_async_copy(src, dst, in_sem.at[n])
        for n, (src, dst) in enumerate(
            (
                (prior_h, prior_b),
                (coup_h, coup_b),
                (cross_h, cross_b),
                (diag_h, diag_b),
                (rhs_h, rhs_b),
                (pix_h, pix_b),
            )
        )
    ]
    for load in loads:
        load.start()

    barrier = pltpu.get_barrier_semaphore()

    def greet_gran(k, carry):
        pl.semaphore_signal(
            barrier, inc=1, device_id=(lax.rem(me + k, NG), mb), device_id_type=MESH
        )
        return carry

    lax.fori_loop(1, NG, greet_gran, 0)
    for k in range(1, NB):
        pl.semaphore_signal(
            barrier, inc=1, device_id=(me, lax.rem(mb + k, NB)), device_id_type=MESH
        )

    lane128 = iota((128, 128), 1)
    sub128 = iota((128, 128), 0)
    gather_table = ((sub128 % 64) // 8 == lane128 % 8).astype(F32).astype(BF16)
    spread_table = ((lane128 % 64) // 8 == sub128 % 8).astype(F32).astype(BF16)
    block32 = iota((32, 128), 1) // 8

    loads[0].wait()

    def take_prior(i, carry):
        for b in range(BD_):
            for v in range(4):
                g0 = prior_b[i, b, pl.ds(2 * v, 8, stride=8), :]
                g1 = prior_b[i, b, pl.ds(2 * v + 1, 8, stride=8), :]
                grids[0, REACH + i, b, 0, v] = g0
                grids[0, REACH + i, b, 1, v] = g1
                resp[REACH + i, b, v] = g0 + g1
        return carry

    lax.fori_loop(0, GD, take_prior, 0)

    def first_halo(k, carry):
        i = edge_granule(k)
        side = 1 - k // 4
        e = lax.rem(k, 4)
        for b in range(BD_):
            halo_out[0, side, 0, e, b] = resp[REACH + i, b].reshape(32, 128).astype(BF16)
            halo_out[0, side, 1, e, b] = grids[0, REACH + i, b, 0].reshape(32, 128).astype(BF16)
        return carry

    lax.fori_loop(0, 8, first_halo, 0)

    pl.semaphore_wait(barrier, NG - 1 + NB - 1)

    def halo_copy(sweep, side, piece):
        return pltpu.make_async_remote_copy(
            src_ref=halo_out.at[sweep, side, piece],
            dst_ref=halo_in.at[sweep, side, piece],
            send_sem=hs_sem.at[sweep, side, piece],
            recv_sem=hr_sem.at[sweep, side, piece],
            device_id=(right if side == 0 else left, mb),
            device_id_type=MESH,
        )

    def start_halo(sweep):
        for piece in range(2):
            for side in range(2):
                halo_copy(sweep, side, piece).start()

    def part_copy(sweep, part, k):
        return pltpu.make_async_remote_copy(
            src_ref=part_out.at[sweep, part],
            dst_ref=part_in.at[sweep, part, k - 1],
            send_sem=ps_sem.at[sweep, part, k - 1],
            recv_sem=pr_sem.at[sweep, part, k - 1],
            device_id=(me, lax.rem(mb + k, NB)),
            device_id_type=MESH,
        )

    start_halo(0)

    slot = (iota((32, 128), 1) // 64) * 4 + iota((32, 128), 0) // 8
    for part, granule_of in ((0, inner_granule), (1, edge_granule)):
        counts = jnp.zeros((32, 128), I32)
        for k in range(8):
            counts = jnp.where(block32 % 8 == k, cnt_s[granule_of(k)], counts)
        weight[part] = (slot < counts).astype(F32)

    def disparity(part, sweep):
        granule_of = (inner_granule, edge_granule)[part]

        def one(k, carry):
            i = granule_of(k)
            own = [resp[REACH + i, b] for b in range(BD_)]
            for s in range(SLOTS):
                n = REACH + i + off_s[s, i]
                total = None
                for b in range(BD_):
                    diff = own[b] - resp[n, b]
                    square = diff * diff
                    total = square if total is None else total + square
                disp[pl.ds(pl.multiple_of(k * 64 + s * 8, 8), 8), :] = (
                    total[0] + total[1] + total[2] + total[3]
                )
            return carry

        lax.fori_loop(0, 8, one, 0)
        sums = split_dot(disp[...], gather_table)
        packed = jnp.zeros((32, 128), F32)
        for k in range(8):
            for h in range(2):
                rows = sums[k * 64 + h * 32 : k * 64 + h * 32 + 32]
                packed = jnp.where(block32 == h * 8 + k, rows, packed)
        part_out[sweep, part] = packed
        for k in (2, 1, 3):
            part_copy(sweep, part, k).start()

    def solve(part, sweep):
        granule_of = (inner_granule, edge_granule)[part]
        now, later = sweep % 2, (sweep + 1) % 2
        last = sweep == SWEEPS - 1
        for k in range(1, NB):
            part_copy(sweep, part, k).wait_recv()
        total = part_out[sweep, part]
        for k in range(NB - 1):
            total = total + part_in[sweep, part, k]
        robust = weight[part] / (1.0 + total * (1.0 / ROBUST))
        rows = []
        for k in range(8):
            for h in range(2):
                rows.append(jnp.where(block32 == h * 8 + k, robust, 0.0))
        spread[...] = split_dot(jnp.concatenate(rows, axis=0), spread_table)

        def one(k, carry):
            i = granule_of(k)
            places = [REACH + i + off_s[s, i] for s in range(SLOTS)]
            for b in range(BD_):
                sigma = drive0 = drive1 = None
                for s in range(SLOTS):
                    rob = spread[pl.ds(pl.multiple_of(k * 64 + s * 8, 8), 8), :]
                    eff = rob[None] * coup[i, b, s]
                    add0 = eff * grids[now, places[s], b, 0]
                    add1 = eff * grids[now, places[s], b, 1]
                    if s == 0:
                        sigma, drive0, drive1 = eff, add0, add1
                    else:
                        sigma, drive0, drive1 = sigma + eff, drive0 + add0, drive1 + add1
                for v in range(4):
                    even = pl.ds(2 * v, 8, stride=8)
                    odd = pl.ds(2 * v + 1, 8, stride=8)
                    r0 = rhs_b[i, b, even, :] + drive0[v]
                    r1 = rhs_b[i, b, odd, :] + drive1[v]
                    first = diag_b[i, b, even, :] + sigma[v]
                    second = diag_b[i, b, odd, :] + sigma[v]
                    cross = cterm[i, b, v]
                    inverse = 1.0 / (first * second - cross * cross)
                    g0 = (second * r0 - cross * r1) * inverse
                    g1 = (first * r1 - cross * r0) * inverse
                    if last:
                        out_b[i, b, even, :] = g0
                        out_b[i, b, odd, :] = g1
                    else:
                        grids[later, REACH + i, b, 0, v] = g0
                        grids[later, REACH + i, b, 1, v] = g1
                        resp[REACH + i, b, v] = g0 + g1
                if part == 1 and not last:
                    side = 1 - k // 4
                    e = lax.rem(k, 4)
                    halo_out[sweep + 1, side, 0, e, b] = (
                        resp[REACH + i, b].reshape(32, 128).astype(BF16)
                    )
                    halo_out[sweep + 1, side, 1, e, b] = (
                        grids[later, REACH + i, b, 0].reshape(32, 128).astype(BF16)
                    )
            return carry

        lax.fori_loop(0, 8, one, 0)
        if part == 1 and not last:
            start_halo(sweep + 1)

    def take_responses(sweep):
        for side in range(2):
            halo_copy(sweep, side, 0).wait_recv()

            def one(e, carry, side=side):
                for b in range(BD_):
                    value = halo_in[sweep, side, 0, e, b].astype(F32)
                    resp[e + side * (REACH + GD), b] = value.reshape(4, 8, 128)
                return carry

            lax.fori_loop(0, REACH, one, 0)

    def take_grids(sweep):
        now = sweep % 2
        for side in range(2):
            halo_copy(sweep, side, 1).wait_recv()

            def one(e, carry, side=side):
                place = e + side * (REACH + GD)
                for b in range(BD_):
                    g0 = halo_in[sweep, side, 1, e, b].astype(F32).reshape(4, 8, 128)
                    grids[now, place, b, 0] = g0
                    grids[now, place, b, 1] = resp[place, b] - g0
                return carry

            lax.fori_loop(0, REACH, one, 0)

    def take_coupling():
        row = iota((256, 256), 0)
        source = (4 * (row % 8) + (row // 8) % 4) * 8 + row // 32
        order = (iota((256, 256), 1) == source).astype(F32).astype(BF16)

        def one(i, carry):
            for b in range(BD_):
                coup[i, b] = dot(order, coup_b[i, b]).reshape(8, 4, 8, 128)
            return carry

        lax.fori_loop(0, GD, one, 0)

    def take_cross():
        def one(half, carry):
            for g in range(8):
                i = half * 8 + g
                for b in range(BD_):
                    for v in range(4):
                        d0 = diag_b[i, b, pl.ds(2 * v, 8, stride=8), :]
                        d1 = diag_b[i, b, pl.ds(2 * v + 1, 8, stride=8), :]
                        value = cross_b[b, half, pl.ds(8 * v + g, 8, stride=32), :]
                        cterm[i, b, v] = value * jnp.sqrt(d0 * d1)
            return carry

        lax.fori_loop(0, 2, one, 0)

    def send_table():
        block = pl.multiple_of((me // 8) * 128, 128)
        turn = lax.rem(128 - lax.rem(me, 8) * 16, 128)
        lane = iota((32, 128), 1)
        tile = iota((32, 128), 0)

        def own(ref_rows):
            pair = []
            for route in range(2):
                row = jnp.broadcast_to(ref_rows(route, pl.ds(block, 128)), (32, 128))
                row = pltpu.roll(row, turn, axis=1)
                pair.append(pltpu.roll(row, 16, axis=1) if route else row)
            return jnp.where(lane < 16, pair[0], pair[1])

        routes = own(lambda route, cols: route_v[pl.ds(route, 1), cols])
        starts = [
            own(lambda route, cols, c=c: win_v[route, pl.ds(c, 1), cols]) for c in range(2)
        ]
        match = (routes == tile) & (lane < 32)
        low = butterfly(jnp.where(match, lane, 99), lane, 32, jnp.minimum)
        high = butterfly(jnp.where(match, lane, -1), lane, 32, jnp.maximum)
        table = jnp.zeros((32, 128), I32)
        for rank, chosen in enumerate((low, high)):
            picks = [
                butterfly(
                    jnp.where((lane == chosen) & (lane < 32), start, 0), lane, 32, jnp.add
                )
                for start in starts
            ]
            valid = (chosen >= 0) & (chosen < 32)
            granule = jnp.where(valid, chosen % 16, 0)
            first = [jnp.clip(pick // SP - 1, 0, FIRST_MAX) for pick in picks]
            for column, value in enumerate((granule, first[0] // 2, first[1])):
                table = jnp.where(lane == rank * 3 + column, value, table)
        tab_v[...] = table
        copy = pltpu.make_async_copy(tab_v, tab_s, tab_sem)
        copy.start()
        copy.wait()

    def weights():
        lane = iota((8, 512), 1)
        place = lane % 16
        match = []
        for route in range(2):
            row = jnp.broadcast_to(route_v[pl.ds(route, 1), :], (8, 512))
            match.append(row == me)
        low = jnp.minimum(
            jnp.where(match[0], place, 99), jnp.where(match[1], place + 16, 99)
        )
        high = jnp.maximum(
            jnp.where(match[0], place, -1), jnp.where(match[1], place + 16, -1)
        )
        low = butterfly(low, lane, 16, jnp.minimum)
        high = butterfly(high, lane, 16, jnp.maximum)
        total = jnp.sum(
            (match[0].astype(F32) + match[1].astype(F32))[0:1], axis=1, keepdims=True
        )
        for rank, chosen in enumerate((low, high)):
            live = (chosen < 32) if rank == 0 else (high != low) & (chosen >= 0)
            for coord, ref in enumerate((roww, colw)):
                pick = jnp.zeros((8, 512), I32)
                for route in range(2):
                    row = jnp.broadcast_to(win_v[route, pl.ds(coord, 1), :], (8, 512))
                    pick = pick + jnp.where(chosen == place + 16 * route, row, 0)
                pick = butterfly(pick, lane, 16, jnp.add)
                first = jnp.clip(pick // SP - 1, 0, FIRST_MAX)
                if coord == 0:
                    knot = (first // 2) * 2 + 2 * (place % 8) + place // 8
                else:
                    knot = first + place
                knot_f = knot.astype(F32)
                extra = jnp.where(
                    knot == 0, -1.0, jnp.where(knot == 63, 64.0, FAR)
                )
                start = pick.astype(F32) * (1.0 / SP)
                lead = start - knot_f
                lead_extra = start - extra

                def rows(block, carry, ref=ref, rank=rank, lead=lead, lead_extra=lead_extra,
                         live=live, coord=coord):
                    parts = []
                    for h in range(2):
                        pixel = (
                            iota((8, 512), 0) + (block * 16 + h * 8)
                        ).astype(F32) * (1.0 / SP)
                        d = jnp.abs(lead + pixel)
                        w = jnp.where(d <= 1.0, near_tap(d), far_tap(d))
                        w = jnp.where(d < 2.0, w, 0.0)
                        d2 = jnp.abs(lead_extra + pixel)
                        w = w + jnp.where(d2 < 2.0, far_tap(d2), 0.0)
                        if coord == 1:
                            w = jnp.where(live, w, 0.0)
                        parts.append(w)
                    ref[pl.ds(pl.multiple_of(block * 16, 16), 16), rank * 512 : rank * 512 + 512] = (
                        jnp.concatenate(parts, axis=0).astype(BF16)
                    )
                    return carry

                lax.fori_loop(0, PIX // 16, rows, 0)
        return 1.0 / total

    def clear_diagonal():
        def one(n, carry):
            diagonal[n] = jnp.zeros((256, 256), BF16)
            return carry

        lax.fori_loop(0, 24, one, 0)

    disparity(0, 0)
    loads[1].wait()
    take_coupling()
    take_responses(0)
    disparity(1, 0)
    loads[2].wait()
    loads[3].wait()
    take_cross()
    take_grids(0)
    loads[4].wait()
    solve(0, 0)
    solve(1, 0)

    disparity(0, 1)
    send_table()
    inverse_cover = weights()
    take_responses(1)
    disparity(1, 1)
    take_grids(1)
    solve(0, 1)
    solve(1, 1)

    disparity(0, 2)
    clear_diagonal()
    take_responses(2)
    disparity(1, 2)
    take_grids(2)
    solve(0, 2)
    solve(1, 2)

    save = pltpu.make_async_copy(out_b, bal_h, out_sem.at[0])
    save.start()

    lane8 = iota((8, 128), 1)
    lane_band = (lane8 % 64) // 16

    def fill(t, carry):
        for rank in range(2):
            granule = tab_s[t, rank * 3]
            row = tab_s[t, rank * 3 + 1]
            column = tab_s[t, rank * 3 + 2]
            halves = []
            for c in range(2):
                value = None
                for b in range(BD_):
                    x = out_b[granule, b, pl.ds(2 * row + c, 8, stride=2), :]
                    x = pltpu.roll(x, lax.rem(b * 16 + 128 - column, 128), axis=1)
                    value = x if value is None else jnp.where(lane_band == b, x, value)
                halves.append(value)
            pay_out[t, rank * 16 : rank * 16 + 16, :] = jnp.concatenate(halves, axis=0).astype(BF16)
        return carry

    lax.fori_loop(0, NG, fill, 0)

    def pay_copy(k):
        return pltpu.make_async_remote_copy(
            src_ref=pay_out.at[lax.rem(me + k, NG)],
            dst_ref=pay_in.at[me],
            send_sem=as_sem.at[k],
            recv_sem=ar_sem.at[k],
            device_id=(lax.rem(me + k, NG), mb),
            device_id_type=MESH,
        )

    def send_pay(k, carry):
        pay_copy(k).start()
        return carry

    lax.fori_loop(1, NG, send_pay, 0)
    own_copy = pltpu.make_async_copy(pay_out.at[me], pay_in.at[me], own_sem)
    own_copy.start()
    loads[5].wait()
    own_copy.wait()

    def take_pay(k, carry):
        pltpu.make_async_remote_copy(
            src_ref=pay_out.at[lax.rem(me + k, NG)],
            dst_ref=pay_in.at[lax.rem(me + NG - k, NG)],
            send_sem=as_sem.at[k],
            recv_sem=ar_sem.at[k],
            device_id=(lax.rem(me + k, NG), mb),
            device_id_type=MESH,
        ).wait_recv()
        return carry

    lax.fori_loop(1, NG, take_pay, 0)

    def expand(group, carry):
        rank = group // 2
        base = lax.rem(group, 2) * 16
        for s in range(16):
            block = pay_in[base + s, pl.ds(pl.multiple_of(rank * 16, 16), 16), :].astype(F32)
            for c in range(2):
                x = block[c * 8 : c * 8 + 8]
                for b in range(BD_):
                    parts = []
                    for parity in range(2):
                        turn = ((s % 8) * 16 - parity * 64 - b * 16) % 128
                        y = pltpu.roll(x, turn, axis=1) if turn else x
                        parts.append(jnp.where(lane8 // 16 == s % 8, y, 0.0))
                    diagonal[
                        group * 6 + b * 2 + c,
                        s * 16 : s * 16 + 16,
                        (s // 8) * 128 : (s // 8) * 128 + 128,
                    ] = jnp.concatenate(parts, axis=0).astype(BF16)
        return carry

    lax.fori_loop(0, 4, expand, 0)

    def correct(b, carry):
        fields = []
        for c in range(2):
            for group in range(4):
                cols = slice(group * 256, group * 256 + 256)
                rowpass[:, cols] = dot(roww[:, cols], diagonal[group * 6 + b * 2 + c]).astype(BF16)
            fields.append(
                lax.dot_general(
                    rowpass[...],
                    colw[...],
                    (((1,), (1,)), ((), ())),
                    preferred_element_type=F32,
                )
            )
        pixels = pix_b[b].astype(F32)
        value = pixels * (1.0 + fields[0] * inverse_cover) + fields[1] * inverse_cover
        tile_b[b] = value.astype(BF16)
        return carry

    lax.fori_loop(0, BD_, correct, 0)
    tiles = pltpu.make_async_copy(tile_b, tile_h, out_sem.at[1])
    tiles.start()

    for sweep in range(SWEEPS):
        for side in range(2):
            for piece in range(2):
                halo_copy(sweep, side, piece).wait_send()
        for part in range(2):
            for k in range(1, NB):
                part_copy(sweep, part, k).wait_send()

    def sent_pay(k, carry):
        pay_copy(k).wait_send()
        return carry

    lax.fori_loop(1, NG, sent_pay, 0)
    save.wait()
    tiles.wait()


def per_device(
    prior_grids,
    pif_rhs,
    pif_diagonal,
    pif_cross,
    pif_coupling,
    neighbour_offset,
    neighbour_count,
    tile_route,
    tile_window,
    tile_pixels,
):
    def pairs(x):
        return x.reshape(GD, BD_, 2, 32, 128).transpose(0, 1, 3, 2, 4).reshape(GD, BD_, 64, 128)

    prior = pairs(prior_grids)
    rhs = pairs(pif_rhs)
    diag = pairs(pif_diagonal)
    cross = (
        pif_cross.reshape(2, 8, BD_, 32, 128).transpose(2, 0, 3, 1, 4).reshape(BD_, 2, 256, 128)
    )
    coupling = (
        pif_coupling.reshape(GD, SLOTS, BD_, 32, 128)
        .transpose(0, 2, 3, 1, 4)
        .reshape(GD, BD_, 256, 128)
    )
    any_ = pl.BlockSpec(memory_space=pl.ANY)
    vmem = pl.BlockSpec(memory_space=pltpu.VMEM)
    smem = pl.BlockSpec(memory_space=pltpu.SMEM)
    dma = pltpu.SemaphoreType.DMA
    balanced, tiles = pl.pallas_call(
        kernel,
        out_shape=(
            jax.ShapeDtypeStruct((GD, BD_, 64, 128), F32),
            jax.ShapeDtypeStruct((BD_, PIX, PIX), BF16),
        ),
        in_specs=[smem, smem, any_, any_, any_, any_, any_, vmem, vmem, any_],
        out_specs=(any_, any_),
        scratch_shapes=[
            pltpu.VMEM((GD, BD_, 64, 128), F32),
            pltpu.VMEM((GD, BD_, 64, 128), F32),
            pltpu.VMEM((GD, BD_, 64, 128), F32),
            pltpu.VMEM((BD_, 2, 256, 128), F32),
            pltpu.VMEM((GD, BD_, 256, 128), BF16),
            pltpu.VMEM((BD_, PIX, PIX), BF16),
            pltpu.VMEM((GD, BD_, 64, 128), F32),
            pltpu.VMEM((BD_, PIX, PIX), BF16),
            pltpu.VMEM((2, GD + 2 * REACH, BD_, 2, 4, 8, 128), F32),
            pltpu.VMEM((GD + 2 * REACH, BD_, 4, 8, 128), F32),
            pltpu.VMEM((GD, BD_, SLOTS, 4, 8, 128), F32),
            pltpu.VMEM((GD, BD_, 4, 8, 128), F32),
            pltpu.VMEM((512, 128), F32),
            pltpu.VMEM((512, 128), F32),
            pltpu.VMEM((2, 32, 128), F32),
            pltpu.VMEM((SWEEPS, 2, 2, REACH, BD_, 32, 128), BF16),
            pltpu.VMEM((SWEEPS, 2, 2, REACH, BD_, 32, 128), BF16),
            pltpu.VMEM((SWEEPS, 2, 32, 128), F32),
            pltpu.VMEM((SWEEPS, 2, NB - 1, 32, 128), F32),
            pltpu.VMEM((NG, 128), I32),
            pltpu.SMEM((NG, 128), I32),
            pltpu.VMEM((NG, 32, 128), BF16),
            pltpu.VMEM((NG, 32, 128), BF16),
            pltpu.VMEM((PIX, 1024), BF16),
            pltpu.VMEM((PIX, 1024), BF16),
            pltpu.VMEM((24, 256, 256), BF16),
            pltpu.VMEM((PIX, 1024), BF16),
            dma((6,)),
            dma((2,)),
            dma((SWEEPS, 2, 2)),
            dma((SWEEPS, 2, 2)),
            dma((SWEEPS, 2, NB - 1)),
            dma((SWEEPS, 2, NB - 1)),
            dma((NG,)),
            dma((NG,)),
            dma,
            dma,
        ],
        compiler_params=pltpu.CompilerParams(
            collective_id=0, has_side_effects=True, vmem_limit_bytes=60 * 1024 * 1024
        ),
        name="balance",
    )(
        neighbour_offset.T,
        neighbour_count,
        prior,
        rhs,
        diag,
        cross,
        coupling,
        tile_route.T,
        tile_window.transpose(1, 2, 0),
        tile_pixels[0],
    )
    balanced = (
        balanced.reshape(GD, BD_, 32, 2, 128)
        .transpose(0, 1, 3, 2, 4)
        .reshape(GD, BD_, 2, 4096)
    )
    return (balanced, tiles[None])


def solution(mesh):
    placed = (
        P("gran", "band", None, None),
        P("gran", "band", None, None),
        P("gran", "band", None, None),
        P("gran", "band", None),
        P("gran", None, "band", None),
        P("gran", None),
        P("gran"),
        P(),
        P(),
        P("gran", "band", None, None),
    )
    return jax.shard_map(
        per_device,
        mesh=mesh,
        in_specs=placed,
        out_specs=(P("gran", "band", None, None), P("gran", "band", None, None)),
        check_vma=False,
    )
```

profile of v0, /device:TPU:1, one launch (start us, length us, event | category | flops | bytes accessed | tf_op | source)
XLA Modules:
  0.0 58.0 jit_solution(6817910676593820743)
XLA Ops:
  0.6 53.8 %balance.1 = (f32[16,3,64,128]{3,2,1,0:T(8,128)}, bf16[3,256,256]{2,1,0:T(8,128)(2,1)}) custom-call(s32[8,16]{1,0:T(8,128)} %bitcast.44, s32[16]{0:T(128)} %cnt_s.1, f32[16,3,64,128]{3,2,1,0:T(8,128)} %bitcast.36, f32[16,3,64,128]{3,2,1,0:T(8,128)} %bitcast.37, f32[16,3,64,128]{3,2,1,0:T(8,128)} %bitcast.38, f32[3,2,256,128]{3,2,1,0:T(8,128)} %bitcast.40, ...), custom_call_target="tpu_custom_call" | custom-call | tf_op jit(solution)/shard_map/balance/pallas_call | solution.py:660
  54.4 0.0 copy-start
  54.4 2.8 %copy.18 = f32[16,3,2,4096]{3,2,1,0:T(2,128)} copy(f32[16,3,2,4096]{3,2,1,0:T(2,128)} %bitcast.39) | data formatting | bytes 3145728
  57.2 0.0 copy-done
  57.2 0.7 %copy.19 = bf16[1,3,256,256]{3,2,1,0:T(8,128)(2,1)} copy(bf16[1,3,256,256]{3,2,1,0:T(8,128)(2,1)S(1)} %bitcast.42) | data formatting | bytes 786432
Async XLA Ops:
  54.4 2.8 %copy-start = (bf16[3,256,256]{2,1,0:T(8,128)(2,1)S(1)}, bf16[3,256,256]{2,1,0:T(8,128)(2,1)}, u32[]{:S(2)}) copy-start(bf16[3,256,256]{2,1,0:T(8,128)(2,1)} %get-tuple-element.5) | copy-start | bytes 1179652
where the time goes:
time: 58.1 us; the launch traced here: 58 us
  Pallas kernels  53.8 us (93%)
  local copies, waits for them, and re-layouts  3.53 us (6%)
  between operations  0.65 us (1%)
    pallas_call x1, Pallas kernels, per_device(): pl.pallas_call(kernel, out_shape=(jax.ShapeDtypeStruct((GD, BD_, 64, 128)...  53.8 us
    unnamed x4, local copies, waits for them, and re-layouts  3.53 us

commit v1 on v0

--- a/solution.py
+++ b/solution.py
@@ -26,6 +26,7 @@
 WIN = 16
 FIRST_MAX = 64 - WIN
 FAR = 1000.0
+FAR_STEPS = 4
 
 
 def iota(shape, dim):
@@ -34,12 +35,6 @@
 
 def dot(a, b):
     return jnp.dot(a, b, preferred_element_type=F32)
-
-
-def split_dot(x, table):
-    high = x.astype(BF16)
-    low = (x - high.astype(F32)).astype(BF16)
-    return dot(high, table) + dot(low, table)
 
 
 def butterfly(x, lane, width, op):
@@ -64,27 +59,32 @@
     return (1.5 * d - 2.5) * d * d + 1.0
 
 
-def edge_granule(k):
-    return k + (k // 4) * 8
-
-
-def inner_granule(k):
-    return k + 4
+PARTS = ((4, 8), (0, 4), (12, 4))
+
+
+def packing(part):
+    count = PARTS[part][1]
+    blocks = 16 // count
+    return count, blocks, 64 // blocks
 
 
 def kernel(
-    off_s,
-    cnt_s,
+    off_h,
+    cnt_h,
     prior_h,
     rhs_h,
     diag_h,
     cross_h,
     coup_h,
-    route_v,
-    win_v,
+    route_h,
+    win_h,
     pix_h,
     bal_h,
     tile_h,
+    off_s,
+    cnt_s,
+    route_v,
+    win_v,
     prior_b,
     rhs_b,
     diag_b,
@@ -122,51 +122,61 @@
     ar_sem,
     tab_sem,
     own_sem,
+    far_sem,
 ):
     me = lax.axis_index("gran")
     mb = lax.axis_index("band")
     right = lax.rem(me + 1, NG)
     left = lax.rem(me + NG - 1, NG)
 
-    loads = [
-        pltpu.make_async_copy(src, dst, in_sem.at[n])
-        for n, (src, dst) in enumerate(
-            (
-                (prior_h, prior_b),
-                (coup_h, coup_b),
-                (cross_h, cross_b),
-                (diag_h, diag_b),
-                (rhs_h, rhs_b),
-                (pix_h, pix_b),
-            )
-        )
-    ]
-    for load in loads:
-        load.start()
-
     barrier = pltpu.get_barrier_semaphore()
-
-    def greet_gran(k, carry):
-        pl.semaphore_signal(
-            barrier, inc=1, device_id=(lax.rem(me + k, NG), mb), device_id_type=MESH
-        )
-        return carry
-
-    lax.fori_loop(1, NG, greet_gran, 0)
+    for other in (left, right):
+        pl.semaphore_signal(barrier, inc=1, device_id=(other, mb), device_id_type=MESH)
     for k in range(1, NB):
         pl.semaphore_signal(
             barrier, inc=1, device_id=(me, lax.rem(mb + k, NB)), device_id_type=MESH
         )
 
+    def far_signal(step):
+        distance = 1 << step
+        for side, shift in enumerate((distance, NG - distance)):
+            pl.semaphore_signal(
+                far_sem.at[step, side],
+                inc=1,
+                device_id=(lax.rem(me + shift, NG), mb),
+                device_id_type=MESH,
+            )
+
+    def far_wait(step):
+        for side in range(2):
+            pl.semaphore_wait(far_sem.at[step, side], 1)
+
+    ends = (pl.ds(0, REACH), pl.ds(GD - REACH, REACH))
+    middle = pl.ds(REACH, GD - 2 * REACH)
+    pairs = [(prior_h.at[part], prior_b.at[part]) for part in (*ends, middle)]
+    pairs += [
+        (off_h, off_s),
+        (cnt_h, cnt_s),
+        (coup_h, coup_b),
+        (diag_h, diag_b),
+        (cross_h, cross_b),
+        (rhs_h, rhs_b),
+        (route_h, route_v),
+        (win_h, win_v),
+        (pix_h, pix_b),
+    ]
+    loads = [
+        pltpu.make_async_copy(src, dst, in_sem.at[n]) for n, (src, dst) in enumerate(pairs)
+    ]
+    for load in loads[:2]:
+        load.start()
+
     lane128 = iota((128, 128), 1)
     sub128 = iota((128, 128), 0)
     gather_table = ((sub128 % 64) // 8 == lane128 % 8).astype(F32).astype(BF16)
     spread_table = ((lane128 % 64) // 8 == sub128 % 8).astype(F32).astype(BF16)
-    block32 = iota((32, 128), 1) // 8
-
-    loads[0].wait()
-
-    def take_prior(i, carry):
+
+    def take_prior(i):
         for b in range(BD_):
             for v in range(4):
                 g0 = prior_b[i, b, pl.ds(2 * v, 8, stride=8), :]
@@ -174,22 +184,28 @@
                 grids[0, REACH + i, b, 0, v] = g0
                 grids[0, REACH + i, b, 1, v] = g1
                 resp[REACH + i, b, v] = g0 + g1
-        return carry
-
-    lax.fori_loop(0, GD, take_prior, 0)
-
-    def first_halo(k, carry):
-        i = edge_granule(k)
-        side = 1 - k // 4
-        e = lax.rem(k, 4)
+
+    def halo_rows(sweep, side, e, i):
         for b in range(BD_):
-            halo_out[0, side, 0, e, b] = resp[REACH + i, b].reshape(32, 128).astype(BF16)
-            halo_out[0, side, 1, e, b] = grids[0, REACH + i, b, 0].reshape(32, 128).astype(BF16)
-        return carry
-
-    lax.fori_loop(0, 8, first_halo, 0)
-
-    pl.semaphore_wait(barrier, NG - 1 + NB - 1)
+            halo_out[sweep, side, 0, e, b] = resp[REACH + i, b].reshape(32, 128).astype(BF16)
+            halo_out[sweep, side, 1, e, b] = (
+                grids[sweep % 2, REACH + i, b, 0].reshape(32, 128).astype(BF16)
+            )
+
+    for load in loads[:2]:
+        load.wait()
+    for load in loads[2:]:
+        load.start()
+    for side, base in ((1, 0), (0, GD - REACH)):
+
+        def first_halo(e, carry, side=side, base=base):
+            take_prior(base + e)
+            halo_rows(0, side, e, base + e)
+            return carry
+
+        lax.fori_loop(0, REACH, first_halo, 0)
+
+    pl.semaphore_wait(barrier, 2 + NB - 1)
 
     def halo_copy(sweep, side, piece):
         return pltpu.make_async_remote_copy(
@@ -201,35 +217,48 @@
             device_id_type=MESH,
         )
 
-    def start_halo(sweep):
+    def start_halo(sweep, side):
         for piece in range(2):
-            for side in range(2):
-                halo_copy(sweep, side, piece).start()
+            halo_copy(sweep, side, piece).start()
 
     def part_copy(sweep, part, k):
         return pltpu.make_async_remote_copy(
-            src_ref=part_out.at[sweep, part],
-            dst_ref=part_in.at[sweep, part, k - 1],
+            src_ref=part_out.at[sweep, part, pl.ds(0, packing(part)[2])],
+            dst_ref=part_in.at[sweep, part, k - 1, pl.ds(0, packing(part)[2])],
             send_sem=ps_sem.at[sweep, part, k - 1],
             recv_sem=pr_sem.at[sweep, part, k - 1],
             device_id=(me, lax.rem(mb + k, NB)),
             device_id_type=MESH,
         )
 
-    start_halo(0)
-
-    slot = (iota((32, 128), 1) // 64) * 4 + iota((32, 128), 0) // 8
-    for part, granule_of in ((0, inner_granule), (1, edge_granule)):
-        counts = jnp.zeros((32, 128), I32)
-        for k in range(8):
-            counts = jnp.where(block32 % 8 == k, cnt_s[granule_of(k)], counts)
-        weight[part] = (slot < counts).astype(F32)
+    start_halo(0, 0)
+    start_halo(0, 1)
+    far_signal(0)
+
+    for load in loads[2:5]:
+        load.wait()
+
+    def rest(k, carry):
+        take_prior(REACH + k)
+        return carry
+
+    lax.fori_loop(0, GD - 2 * REACH, rest, 0)
+
+    for part in range(3):
+        count, blocks, rows = packing(part)
+        lane_block = iota((rows, 128), 1) // 8
+        slot = (lane_block // count) * (SLOTS // blocks) + iota((rows, 128), 0) // 8
+        counts = jnp.zeros((rows, 128), I32)
+        for k in range(count):
+            counts = jnp.where(lane_block % count == k, cnt_s[PARTS[part][0] + k], counts)
+        weight[part, :rows] = (slot < counts).astype(F32)
 
     def disparity(part, sweep):
-        granule_of = (inner_granule, edge_granule)[part]
+        base = PARTS[part][0]
+        count, blocks, height = packing(part)
 
         def one(k, carry):
-            i = granule_of(k)
+            i = base + k
             own = [resp[REACH + i, b] for b in range(BD_)]
             for s in range(SLOTS):
                 n = REACH + i + off_s[s, i]
@@ -243,35 +272,38 @@
                 )
             return carry
 
-        lax.fori_loop(0, 8, one, 0)
-        sums = split_dot(disp[...], gather_table)
-        packed = jnp.zeros((32, 128), F32)
-        for k in range(8):
-            for h in range(2):
-                rows = sums[k * 64 + h * 32 : k * 64 + h * 32 + 32]
-                packed = jnp.where(block32 == h * 8 + k, rows, packed)
-        part_out[sweep, part] = packed
+        lax.fori_loop(0, count, one, 0)
+        sums = dot(disp[: count * 64].astype(BF16), gather_table)
+        packed = jnp.zeros((height, 128), F32)
+        lane_block = iota((height, 128), 1) // 8
+        for k in range(count):
+            for h in range(blocks):
+                at = k * 64 + h * height
+                packed = jnp.where(lane_block == h * count + k, sums[at : at + height], packed)
+        part_out[sweep, part, :height] = packed.astype(BF16)
         for k in (2, 1, 3):
             part_copy(sweep, part, k).start()
 
     def solve(part, sweep):
-        granule_of = (inner_granule, edge_granule)[part]
+        base = PARTS[part][0]
+        count, blocks, height = packing(part)
         now, later = sweep % 2, (sweep + 1) % 2
         last = sweep == SWEEPS - 1
         for k in range(1, NB):
             part_copy(sweep, part, k).wait_recv()
-        total = part_out[sweep, part]
+        total = part_out[sweep, part, :height].astype(F32)
         for k in range(NB - 1):
-            total = total + part_in[sweep, part, k]
-        robust = weight[part] / (1.0 + total * (1.0 / ROBUST))
+            total = total + part_in[sweep, part, k, :height].astype(F32)
+        robust = weight[part, :height] / (1.0 + total * (1.0 / ROBUST))
+        lane_block = iota((height, 128), 1) // 8
         rows = []
-        for k in range(8):
-            for h in range(2):
-                rows.append(jnp.where(block32 == h * 8 + k, robust, 0.0))
-        spread[...] = split_dot(jnp.concatenate(rows, axis=0), spread_table)
+        for k in range(count):
+            for h in range(blocks):
+                rows.append(jnp.where(lane_block == h * count + k, robust, 0.0))
+        spread[: count * 64] = dot(jnp.concatenate(rows, axis=0).astype(BF16), spread_table)
 
         def one(k, carry):
-            i = granule_of(k)
+            i = base + k
             places = [REACH + i + off_s[s, i] for s in range(SLOTS)]
             for b in range(BD_):
                 sigma = drive0 = drive1 = None
@@ -302,47 +334,38 @@
                         grids[later, REACH + i, b, 0, v] = g0
                         grids[later, REACH + i, b, 1, v] = g1
                         resp[REACH + i, b, v] = g0 + g1
-                if part == 1 and not last:
-                    side = 1 - k // 4
-                    e = lax.rem(k, 4)
-                    halo_out[sweep + 1, side, 0, e, b] = (
-                        resp[REACH + i, b].reshape(32, 128).astype(BF16)
-                    )
-                    halo_out[sweep + 1, side, 1, e, b] = (
-                        grids[later, REACH + i, b, 0].reshape(32, 128).astype(BF16)
-                    )
+            if part > 0 and not last:
+                halo_rows(sweep + 1, 2 - part, k, i)
             return carry
 
-        lax.fori_loop(0, 8, one, 0)
-        if part == 1 and not last:
-            start_halo(sweep + 1)
-
-    def take_responses(sweep):
-        for side in range(2):
-            halo_copy(sweep, side, 0).wait_recv()
-
-            def one(e, carry, side=side):
-                for b in range(BD_):
-                    value = halo_in[sweep, side, 0, e, b].astype(F32)
-                    resp[e + side * (REACH + GD), b] = value.reshape(4, 8, 128)
-                return carry
-
-            lax.fori_loop(0, REACH, one, 0)
-
-    def take_grids(sweep):
+        lax.fori_loop(0, count, one, 0)
+        if part > 0 and not last:
+            start_halo(sweep + 1, 2 - part)
+
+    def take_responses(sweep, side):
+        halo_copy(sweep, side, 0).wait_recv()
+
+        def one(e, carry):
+            for b in range(BD_):
+                value = halo_in[sweep, side, 0, e, b].astype(F32)
+                resp[e + side * (REACH + GD), b] = value.reshape(4, 8, 128)
+            return carry
+
+        lax.fori_loop(0, REACH, one, 0)
+
+    def take_grids(sweep, side):
         now = sweep % 2
-        for side in range(2):
-            halo_copy(sweep, side, 1).wait_recv()
-
-            def one(e, carry, side=side):
-                place = e + side * (REACH + GD)
-                for b in range(BD_):
-                    g0 = halo_in[sweep, side, 1, e, b].astype(F32).reshape(4, 8, 128)
-                    grids[now, place, b, 0] = g0
-                    grids[now, place, b, 1] = resp[place, b] - g0
-                return carry
-
-            lax.fori_loop(0, REACH, one, 0)
+        halo_copy(sweep, side, 1).wait_recv()
+
+        def one(e, carry):
+            place = e + side * (REACH + GD)
+            for b in range(BD_):
+                g0 = halo_in[sweep, side, 1, e, b].astype(F32).reshape(4, 8, 128)
+                grids[now, place, b, 0] = g0
+                grids[now, place, b, 1] = resp[place, b] - g0
+            return carry
+
+        lax.fori_loop(0, REACH, one, 0)
 
     def take_coupling():
         row = iota((256, 256), 0)
@@ -351,10 +374,13 @@
 
         def one(i, carry):
             for b in range(BD_):
-                coup[i, b] = dot(order, coup_b[i, b]).reshape(8, 4, 8, 128)
+                both = jnp.concatenate([coup_b[i, b], coup_b[i + 8, b]], axis=1)
+                moved = dot(order, both)
+                coup[i, b] = moved[:, :128].reshape(SLOTS, 4, 8, 128)
+                coup[i + 8, b] = moved[:, 128:].reshape(SLOTS, 4, 8, 128)
             return carry
 
-        lax.fori_loop(0, GD, one, 0)
+        lax.fori_loop(0, GD // 2, one, 0)
 
     def take_cross():
         def one(half, carry):
@@ -409,7 +435,7 @@
         copy.start()
         copy.wait()
 
-    def weights():
+    def weights(coord, ref):
         lane = iota((8, 512), 1)
         place = lane % 16
         match = []
@@ -429,7 +455,7 @@
         )
         for rank, chosen in enumerate((low, high)):
             live = (chosen < 32) if rank == 0 else (high != low) & (chosen >= 0)
-            for coord, ref in enumerate((roww, colw)):
+            if True:
                 pick = jnp.zeros((8, 512), I32)
                 for route in range(2):
                     row = jnp.broadcast_to(win_v[route, pl.ds(coord, 1), :], (8, 512))
@@ -478,35 +504,42 @@
 
         lax.fori_loop(0, 24, one, 0)
 
-    disparity(0, 0)
-    loads[1].wait()
-    take_coupling()
-    take_responses(0)
-    disparity(1, 0)
-    loads[2].wait()
-    loads[3].wait()
-    take_cross()
-    take_grids(0)
-    loads[4].wait()
-    solve(0, 0)
-    solve(1, 0)
-
-    disparity(0, 1)
-    send_table()
-    inverse_cover = weights()
-    take_responses(1)
-    disparity(1, 1)
-    take_grids(1)
-    solve(0, 1)
-    solve(1, 1)
-
-    disparity(0, 2)
-    clear_diagonal()
-    take_responses(2)
-    disparity(1, 2)
-    take_grids(2)
-    solve(0, 2)
-    solve(1, 2)
+    cover = None
+    for sweep in range(SWEEPS):
+        order = (1, 2) if sweep % 2 == 0 else (2, 1)
+        disparity(0, sweep)
+        if sweep == 0:
+            loads[5].wait()
+            take_coupling()
+        elif sweep == 1:
+            far_wait(1)
+            far_signal(2)
+            loads[9].wait()
+            loads[10].wait()
+            weights(0, roww)
+        else:
+            cover = weights(1, colw)
+        for step, part in enumerate(order):
+            take_responses(sweep, part - 1)
+            if step == 0 and sweep < 2:
+                far_wait(2 * sweep)
+                far_signal(2 * sweep + 1)
+            disparity(part, sweep)
+        if sweep == 0:
+            loads[6].wait()
+            loads[7].wait()
+            take_cross()
+            loads[8].wait()
+        solve(0, sweep)
+        if sweep == 1:
+            send_table()
+        elif sweep == 2:
+            clear_diagonal()
+            far_wait(3)
+        for part in order:
+            take_grids(sweep, part - 1)
+            solve(part, sweep)
+    inverse_cover = cover
 
     save = pltpu.make_async_copy(out_b, bal_h, out_sem.at[0])
     save.start()
@@ -549,7 +582,7 @@
     lax.fori_loop(1, NG, send_pay, 0)
     own_copy = pltpu.make_async_copy(pay_out.at[me], pay_in.at[me], own_sem)
     own_copy.start()
-    loads[5].wait()
+    loads[11].wait()
     own_copy.wait()
 
     def take_pay(k, carry):
@@ -614,7 +647,7 @@
         for side in range(2):
             for piece in range(2):
                 halo_copy(sweep, side, piece).wait_send()
-        for part in range(2):
+        for part in range(3):
             for k in range(1, NB):
                 part_copy(sweep, part, k).wait_send()
 
@@ -654,8 +687,6 @@
         .reshape(GD, BD_, 256, 128)
     )
     any_ = pl.BlockSpec(memory_space=pl.ANY)
-    vmem = pl.BlockSpec(memory_space=pltpu.VMEM)
-    smem = pl.BlockSpec(memory_space=pltpu.SMEM)
     dma = pltpu.SemaphoreType.DMA
     balanced, tiles = pl.pallas_call(
         kernel,
@@ -663,9 +694,13 @@
             jax.ShapeDtypeStruct((GD, BD_, 64, 128), F32),
             jax.ShapeDtypeStruct((BD_, PIX, PIX), BF16),
         ),
-        in_specs=[smem, smem, any_, any_, any_, any_, any_, vmem, vmem, any_],
+        in_specs=[any_] * 10,
         out_specs=(any_, any_),
         scratch_shapes=[
+            pltpu.SMEM((SLOTS, GD), I32),
+            pltpu.SMEM((GD,), I32),
+            pltpu.VMEM((2, NG * GD), I32),
+            pltpu.VMEM((2, 2, NG * GD), I32),
             pltpu.VMEM((GD, BD_, 64, 128), F32),
             pltpu.VMEM((GD, BD_, 64, 128), F32),
             pltpu.VMEM((GD, BD_, 64, 128), F32),
@@ -680,11 +715,11 @@
             pltpu.VMEM((GD, BD_, 4, 8, 128), F32),
             pltpu.VMEM((512, 128), F32),
             pltpu.VMEM((512, 128), F32),
-            pltpu.VMEM((2, 32, 128), F32),
+            pltpu.VMEM((3, 32, 128), F32),
             pltpu.VMEM((SWEEPS, 2, 2, REACH, BD_, 32, 128), BF16),
             pltpu.VMEM((SWEEPS, 2, 2, REACH, BD_, 32, 128), BF16),
-            pltpu.VMEM((SWEEPS, 2, 32, 128), F32),
-            pltpu.VMEM((SWEEPS, 2, NB - 1, 32, 128), F32),
+            pltpu.VMEM((SWEEPS, 3, 32, 128), BF16),
+            pltpu.VMEM((SWEEPS, 3, NB - 1, 32, 128), BF16),
             pltpu.VMEM((NG, 128), I32),
             pltpu.SMEM((NG, 128), I32),
             pltpu.VMEM((NG, 32, 128), BF16),
@@ -693,16 +728,17 @@
             pltpu.VMEM((PIX, 1024), BF16),
             pltpu.VMEM((24, 256, 256), BF16),
             pltpu.VMEM((PIX, 1024), BF16),
-            dma((6,)),
+            dma((12,)),
             dma((2,)),
             dma((SWEEPS, 2, 2)),
             dma((SWEEPS, 2, 2)),
-            dma((SWEEPS, 2, NB - 1)),
-            dma((SWEEPS, 2, NB - 1)),
+            dma((SWEEPS, 3, NB - 1)),
+            dma((SWEEPS, 3, NB - 1)),
             dma((NG,)),
             dma((NG,)),
             dma,
             dma,
+            pltpu.SemaphoreType.REGULAR((FAR_STEPS, 2)),
         ],
         compiler_params=pltpu.CompilerParams(
             collective_id=0, has_side_effects=True, vmem_limit_bytes=60 * 1024 * 1024

time: 58.1 us -> 51.9 us (0.89)
  Pallas kernels: 53.8 us -> 47.5 us
    pallas_call x1, Pallas kernels: 53.8 us -> 47.5 us  [per_device(): pl.pallas_call(kernel, out_shape=(jax.ShapeDtypeStruct((GD, BD_, 64, 128)...]
where the time goes in v1:
time: 51.9 us; the launch traced here: 51.7 us
  Pallas kernels  47.5 us (92%)
  local copies, waits for them, and re-layouts  3.53 us (7%)
  between operations  0.65 us (1%)
    pallas_call x1, Pallas kernels, per_device(): pl.pallas_call(kernel, out_shape=(jax.ShapeDtypeStruct((GD, BD_, 64, 128)...  47.5 us
    unnamed x4, local copies, waits for them, and re-layouts  3.53 us

profile of v1, /device:TPU:1, one launch (start us, length us, event | category | flops | bytes accessed | tf_op | source)
XLA Modules:
  0.0 51.7 jit_solution(2064460709069421457)
XLA Ops:
  0.6 47.5 %balance.1 = (f32[16,3,64,128]{3,2,1,0:T(8,128)}, bf16[3,256,256]{2,1,0:T(8,128)(2,1)}) custom-call(s32[8,16]{1,0:T(8,128)} %bitcast.44, s32[16]{0:T(128)} %cnt_h.1, f32[16,3,64,128]{3,2,1,0:T(8,128)} %bitcast.36, f32[16,3,64,128]{3,2,1,0:T(8,128)} %bitcast.37, f32[16,3,64,128]{3,2,1,0:T(8,128)} %bitcast.38, f32[3,2,256,128]{3,2,1,0:T(8,128)} %bitcast.40, ...), custom_call_target="tpu_custom_call" | custom-call | tf_op jit(solution)/shard_map/balance/pallas_call | solution.py:691
  48.2 0.0 copy-start
  48.2 2.8 %copy.18 = f32[16,3,2,4096]{3,2,1,0:T(2,128)} copy(f32[16,3,2,4096]{3,2,1,0:T(2,128)} %bitcast.39) | data formatting | bytes 3145728
  51.0 0.0 copy-done
  51.0 0.7 %copy.19 = bf16[1,3,256,256]{3,2,1,0:T(8,128)(2,1)} copy(bf16[1,3,256,256]{3,2,1,0:T(8,128)(2,1)S(1)} %bitcast.42) | data formatting | bytes 786432
Async XLA Ops:
  48.2 2.8 %copy-start = (bf16[3,256,256]{2,1,0:T(8,128)(2,1)S(1)}, bf16[3,256,256]{2,1,0:T(8,128)(2,1)}, u32[]{:S(2)}) copy-start(bf16[3,256,256]{2,1,0:T(8,128)(2,1)} %get-tuple-element.5) | copy-start | bytes 1179652

commit v2 on v1

--- a/solution.py
+++ b/solution.py
@@ -27,6 +27,7 @@
 FIRST_MAX = 64 - WIN
 FAR = 1000.0
 FAR_STEPS = 4
+TILE_VMEM = 60 * 1024 * 1024
 
 
 def iota(shape, dim):
@@ -78,9 +79,11 @@
     coup_h,
     route_h,
     win_h,
-    pix_h,
     bal_h,
-    tile_h,
+    pay_in,
+    roww_h,
+    colw_h,
+    cover_h,
     off_s,
     cnt_s,
     route_v,
@@ -90,9 +93,7 @@
     diag_b,
     cross_b,
     coup_b,
-    pix_b,
     out_b,
-    tile_b,
     grids,
     resp,
     coup,
@@ -107,11 +108,10 @@
     tab_v,
     tab_s,
     pay_out,
-    pay_in,
     roww,
     colw,
-    diagonal,
-    rowpass,
+    colt,
+    cover_v,
     in_sem,
     out_sem,
     hs_sem,
@@ -163,7 +163,6 @@
         (rhs_h, rhs_b),
         (route_h, route_v),
         (win_h, win_v),
-        (pix_h, pix_b),
     ]
     loads = [
         pltpu.make_async_copy(src, dst, in_sem.at[n]) for n, (src, dst) in enumerate(pairs)
@@ -208,18 +207,16 @@
     pl.semaphore_wait(barrier, 2 + NB - 1)
 
     def halo_copy(sweep, side, piece):
+        whole = not isinstance(piece, jax.Array) and piece == REACH
+        part = (sweep, side, 1) if whole else (sweep, side, 0, piece)
         return pltpu.make_async_remote_copy(
-            src_ref=halo_out.at[sweep, side, piece],
-            dst_ref=halo_in.at[sweep, side, piece],
+            src_ref=halo_out.at[part],
+            dst_ref=halo_in.at[part],
             send_sem=hs_sem.at[sweep, side, piece],
             recv_sem=hr_sem.at[sweep, side, piece],
             device_id=(right if side == 0 else left, mb),
             device_id_type=MESH,
         )
-
-    def start_halo(sweep, side):
-        for piece in range(2):
-            halo_copy(sweep, side, piece).start()
 
     def part_copy(sweep, part, k):
         return pltpu.make_async_remote_copy(
@@ -231,8 +228,9 @@
             device_id_type=MESH,
         )
 
-    start_halo(0, 0)
-    start_halo(0, 1)
+    for piece in range(REACH + 1):
+        for side in range(2):
+            halo_copy(0, side, piece).start()
     far_signal(0)
 
     for load in loads[2:5]:
@@ -336,16 +334,16 @@
                         resp[REACH + i, b, v] = g0 + g1
             if part > 0 and not last:
                 halo_rows(sweep + 1, 2 - part, k, i)
+                halo_copy(sweep + 1, 2 - part, k).start()
             return carry
 
         lax.fori_loop(0, count, one, 0)
         if part > 0 and not last:
-            start_halo(sweep + 1, 2 - part)
+            halo_copy(sweep + 1, 2 - part, REACH).start()
 
     def take_responses(sweep, side):
-        halo_copy(sweep, side, 0).wait_recv()
-
         def one(e, carry):
+            halo_copy(sweep, side, e).wait_recv()
             for b in range(BD_):
                 value = halo_in[sweep, side, 0, e, b].astype(F32)
                 resp[e + side * (REACH + GD), b] = value.reshape(4, 8, 128)
@@ -355,7 +353,7 @@
 
     def take_grids(sweep, side):
         now = sweep % 2
-        halo_copy(sweep, side, 1).wait_recv()
+        halo_copy(sweep, side, REACH).wait_recv()
 
         def one(e, carry):
             place = e + side * (REACH + GD)
@@ -495,16 +493,14 @@
                     return carry
 
                 lax.fori_loop(0, PIX // 16, rows, 0)
-        return 1.0 / total
-
-    def clear_diagonal():
-        def one(n, carry):
-            diagonal[n] = jnp.zeros((256, 256), BF16)
-            return carry
-
-        lax.fori_loop(0, 24, one, 0)
-
-    cover = None
+        cover_v[...] = jnp.broadcast_to(1.0 / total, (8, 128))
+
+    saves = [
+        pltpu.make_async_copy(src, dst, out_sem.at[n])
+        for n, (src, dst) in enumerate(
+            ((roww, roww_h), (colt, colw_h), (cover_v, cover_h), (out_b, bal_h))
+        )
+    ]
     for sweep in range(SWEEPS):
         order = (1, 2) if sweep % 2 == 0 else (2, 1)
         disparity(0, sweep)
@@ -517,8 +513,12 @@
             loads[9].wait()
             loads[10].wait()
             weights(0, roww)
+            saves[0].start()
         else:
-            cover = weights(1, colw)
+            weights(1, colw)
+            colt[...] = colw[...].T
+            saves[1].start()
+            saves[2].start()
         for step, part in enumerate(order):
             take_responses(sweep, part - 1)
             if step == 0 and sweep < 2:
@@ -534,20 +534,16 @@
         if sweep == 1:
             send_table()
         elif sweep == 2:
-            clear_diagonal()
             far_wait(3)
         for part in order:
             take_grids(sweep, part - 1)
             solve(part, sweep)
-    inverse_cover = cover
-
-    save = pltpu.make_async_copy(out_b, bal_h, out_sem.at[0])
-    save.start()
+    saves[3].start()
 
     lane8 = iota((8, 128), 1)
     lane_band = (lane8 % 64) // 16
 
-    def fill(t, carry):
+    def fill(t):
         for rank in range(2):
             granule = tab_s[t, rank * 3]
             row = tab_s[t, rank * 3 + 1]
@@ -561,9 +557,6 @@
                     value = x if value is None else jnp.where(lane_band == b, x, value)
                 halves.append(value)
             pay_out[t, rank * 16 : rank * 16 + 16, :] = jnp.concatenate(halves, axis=0).astype(BF16)
-        return carry
-
-    lax.fori_loop(0, NG, fill, 0)
 
     def pay_copy(k):
         return pltpu.make_async_remote_copy(
@@ -575,14 +568,21 @@
             device_id_type=MESH,
         )
 
-    def send_pay(k, carry):
-        pay_copy(k).start()
+    def fill_and_send(n, carry):
+        steps = [lax.rem(12 + n * 4 + u, NG) for u in range(4)]
+        for k in steps:
+            fill(lax.rem(me + k, NG))
+        for k in steps:
+
+            @pl.when(k > 0)
+            def _(k=k):
+                pay_copy(k).start()
+
         return carry
 
-    lax.fori_loop(1, NG, send_pay, 0)
+    lax.fori_loop(0, NG // 4, fill_and_send, 0)
     own_copy = pltpu.make_async_copy(pay_out.at[me], pay_in.at[me], own_sem)
     own_copy.start()
-    loads[11].wait()
     own_copy.wait()
 
     def take_pay(k, carry):
@@ -597,6 +597,70 @@
         return carry
 
     lax.fori_loop(1, NG, take_pay, 0)
+
+    for sweep in range(SWEEPS):
+        for side in range(2):
+            for piece in range(REACH + 1):
+                halo_copy(sweep, side, piece).wait_send()
+        for part in range(3):
+            for k in range(1, NB):
+                part_copy(sweep, part, k).wait_send()
+
+    def sent_pay(k, carry):
+        pay_copy(k).wait_send()
+        return carry
+
+    lax.fori_loop(1, NG, sent_pay, 0)
+    for save in saves:
+        save.wait()
+
+
+def tile_kernel(
+    pay_h,
+    roww_h,
+    colw_h,
+    cover_h,
+    pix_h,
+    mid_h,
+    bal_h,
+    tile_h,
+    pay_in,
+    roww,
+    colw,
+    cover,
+    pix_b,
+    bal_b,
+    tile_b,
+    diagonal,
+    rowpass,
+    in_sem,
+    out_sem,
+):
+    quarter = [pl.ds(4 * n, 4) for n in range(4)]
+    pairs = [
+        (pay_h, pay_in),
+        (roww_h, roww),
+        (colw_h, colw),
+        (cover_h, cover),
+        (pix_h, pix_b),
+    ] + [(mid_h.at[part], bal_b.at[part]) for part in quarter]
+    loads = [
+        pltpu.make_async_copy(src, dst, in_sem.at[n]) for n, (src, dst) in enumerate(pairs)
+    ]
+    for load in loads:
+        load.start()
+    saves = [
+        pltpu.make_async_copy(bal_b.at[part], bal_h.at[part], out_sem.at[n])
+        for n, part in enumerate(quarter)
+    ]
+
+    def clear(n, carry):
+        diagonal[n] = jnp.zeros((256, 256), BF16)
+        return carry
+
+    lax.fori_loop(0, 24, clear, 0)
+    lane8 = iota((8, 128), 1)
+    loads[0].wait()
 
     def expand(group, carry):
         rank = group // 2
@@ -620,44 +684,32 @@
 
     lax.fori_loop(0, 4, expand, 0)
 
+    for load in loads[1:4]:
+        load.wait()
+    for load, save in zip(loads[5:], saves):
+        load.wait()
+        save.start()
+    loads[4].wait()
+    inverse_cover = cover[0:1, 0:1]
+
     def correct(b, carry):
         fields = []
         for c in range(2):
             for group in range(4):
                 cols = slice(group * 256, group * 256 + 256)
                 rowpass[:, cols] = dot(roww[:, cols], diagonal[group * 6 + b * 2 + c]).astype(BF16)
-            fields.append(
-                lax.dot_general(
-                    rowpass[...],
-                    colw[...],
-                    (((1,), (1,)), ((), ())),
-                    preferred_element_type=F32,
-                )
-            )
+            fields.append(dot(rowpass[...], colw[...]))
         pixels = pix_b[b].astype(F32)
         value = pixels * (1.0 + fields[0] * inverse_cover) + fields[1] * inverse_cover
         tile_b[b] = value.astype(BF16)
+        pltpu.make_async_copy(tile_b.at[b], tile_h.at[b], out_sem.at[4 + b]).start()
         return carry
 
     lax.fori_loop(0, BD_, correct, 0)
-    tiles = pltpu.make_async_copy(tile_b, tile_h, out_sem.at[1])
-    tiles.start()
-
-    for sweep in range(SWEEPS):
-        for side in range(2):
-            for piece in range(2):
-                halo_copy(sweep, side, piece).wait_send()
-        for part in range(3):
-            for k in range(1, NB):
-                part_copy(sweep, part, k).wait_send()
-
-    def sent_pay(k, carry):
-        pay_copy(k).wait_send()
-        return carry
-
-    lax.fori_loop(1, NG, sent_pay, 0)
-    save.wait()
-    tiles.wait()
+    for save in saves:
+        save.wait()
+    for b in range(BD_):
+        pltpu.make_async_copy(tile_b.at[b], tile_h.at[b], out_sem.at[4 + b]).wait()
 
 
 def per_device(
@@ -688,14 +740,17 @@
     )
     any_ = pl.BlockSpec(memory_space=pl.ANY)
     dma = pltpu.SemaphoreType.DMA
-    balanced, tiles = pl.pallas_call(
+    middle, payload, roww, colw, cover = pl.pallas_call(
         kernel,
         out_shape=(
             jax.ShapeDtypeStruct((GD, BD_, 64, 128), F32),
-            jax.ShapeDtypeStruct((BD_, PIX, PIX), BF16),
+            jax.ShapeDtypeStruct((NG, 32, 128), BF16),
+            jax.ShapeDtypeStruct((PIX, 1024), BF16),
+            jax.ShapeDtypeStruct((1024, PIX), BF16),
+            jax.ShapeDtypeStruct((8, 128), F32),
         ),
-        in_specs=[any_] * 10,
-        out_specs=(any_, any_),
+        in_specs=[any_] * 9,
+        out_specs=(any_,) * 5,
         scratch_shapes=[
             pltpu.SMEM((SLOTS, GD), I32),
             pltpu.SMEM((GD,), I32),
@@ -706,9 +761,7 @@
             pltpu.VMEM((GD, BD_, 64, 128), F32),
             pltpu.VMEM((BD_, 2, 256, 128), F32),
             pltpu.VMEM((GD, BD_, 256, 128), BF16),
-            pltpu.VMEM((BD_, PIX, PIX), BF16),
             pltpu.VMEM((GD, BD_, 64, 128), F32),
-            pltpu.VMEM((BD_, PIX, PIX), BF16),
             pltpu.VMEM((2, GD + 2 * REACH, BD_, 2, 4, 8, 128), F32),
             pltpu.VMEM((GD + 2 * REACH, BD_, 4, 8, 128), F32),
             pltpu.VMEM((GD, BD_, SLOTS, 4, 8, 128), F32),
@@ -723,15 +776,14 @@
             pltpu.VMEM((NG, 128), I32),
             pltpu.SMEM((NG, 128), I32),
             pltpu.VMEM((NG, 32, 128), BF16),
-            pltpu.VMEM((NG, 32, 128), BF16),
             pltpu.VMEM((PIX, 1024), BF16),
             pltpu.VMEM((PIX, 1024), BF16),
-            pltpu.VMEM((24, 256, 256), BF16),
-            pltpu.VMEM((PIX, 1024), BF16),
-            dma((12,)),
-            dma((2,)),
-            dma((SWEEPS, 2, 2)),
-            dma((SWEEPS, 2, 2)),
+            pltpu.VMEM((1024, PIX), BF16),
+            pltpu.VMEM((8, 128), F32),
+            dma((11,)),
+            dma((4,)),
+            dma((SWEEPS, 2, REACH + 1)),
+            dma((SWEEPS, 2, REACH + 1)),
             dma((SWEEPS, 3, NB - 1)),
             dma((SWEEPS, 3, NB - 1)),
             dma((NG,)),
@@ -754,8 +806,31 @@
         coupling,
         tile_route.T,
         tile_window.transpose(1, 2, 0),
-        tile_pixels[0],
     )
+    balanced, tiles = pl.pallas_call(
+        tile_kernel,
+        out_shape=(
+            jax.ShapeDtypeStruct((GD, BD_, 64, 128), F32),
+            jax.ShapeDtypeStruct((BD_, PIX, PIX), BF16),
+        ),
+        in_specs=[any_] * 6,
+        out_specs=(any_, any_),
+        scratch_shapes=[
+            pltpu.VMEM((NG, 32, 128), BF16),
+            pltpu.VMEM((PIX, 1024), BF16),
+            pltpu.VMEM((1024, PIX), BF16),
+            pltpu.VMEM((8, 128), F32),
+            pltpu.VMEM((BD_, PIX, PIX), BF16),
+            pltpu.VMEM((GD, BD_, 64, 128), F32),
+            pltpu.VMEM((BD_, PIX, PIX), BF16),
+            pltpu.VMEM((24, 256, 256), BF16),
+            pltpu.VMEM((PIX, 1024), BF16),
+            dma((9,)),
+            dma((7,)),
+        ],
+        compiler_params=pltpu.CompilerParams(vmem_limit_bytes=TILE_VMEM),
+        name="tiles",
+    )(payload, roww, colw, cover, tile_pixels[0], middle)
     balanced = (
         balanced.reshape(GD, BD_, 32, 2, 128)
         .transpose(0, 1, 3, 2, 4)

time: 51.9 us -> 48 us (0.925)
  local copies, waits for them, and re-layouts: 3.53 us -> 0 us
    pallas_call x1, Pallas kernels: 47.5 us -> 42 us  [per_device(): pl.pallas_call(kernel, out_shape=(jax.ShapeDtypeStruct((GD, BD_, 64, 128)...]
    pallas_call x0 -> x1, Pallas kernels: none -> 5.16 us  [per_device(): pl.pallas_call(tile_kernel, out_shape=(jax.ShapeDtypeStruct((GD, BD_, 64,...]
    unnamed x4 -> x0, local copies, waits for them, and re-layouts: 3.53 us -> none
where the time goes in v2:
time: 48 us; the launch traced here: 47.9 us
  Pallas kernels  47.2 us (98%)
  between operations  0.64 us (1%)
    pallas_call x1, Pallas kernels, per_device(): pl.pallas_call(kernel, out_shape=(jax.ShapeDtypeStruct((GD, BD_, 64, 128)...  42 us
    pallas_call x1, Pallas kernels, per_device(): pl.pallas_call(tile_kernel, out_shape=(jax.ShapeDtypeStruct((GD, BD_, 64,...  5.16 us

profile of v2, /device:TPU:1, one launch (start us, length us, event | category | flops | bytes accessed | tf_op | source)
XLA Modules:
  0.0 47.9 jit_solution(13775480876637421481)
XLA Ops:
  0.6 42.0 %balance.1 = (f32[16,3,64,128]{3,2,1,0:T(8,128)}, bf16[32,32,128]{2,1,0:T(8,128)(2,1)}, bf16[256,1024]{1,0:T(8,128)(2,1)}, bf16[1024,256]{1,0:T(8,128)(2,1)}, f32[8,128]{1,0:T(8,128)}) custom-call(s32[8,16]{1,0:T(8,128)} %bitcast.42, s32[16]{0:T(128)} %cnt_h.1, f32[16,3,64,128]{3,2,1,0:T(8,128)} %bitcast.36, f32[16,3,64,128]{3,2,1,0:T(8,128)} %bitcast.37, ...), custom_call_target="tpu_custom_call" | custom-call | tf_op jit(solution)/shard_map/balance/pallas_call | solution.py:743
  42.7 5.2 %tiles.1 = (f32[16,3,64,128]{3,2,1,0:T(8,128)}, bf16[3,256,256]{2,1,0:T(8,128)(2,1)}) custom-call(bf16[32,32,128]{2,1,0:T(8,128)(2,1)} %get-tuple-element.9.pay_h, bf16[256,1024]{1,0:T(8,128)(2,1)} %get-tuple-element.10.roww_h, bf16[1024,256]{1,0:T(8,128)(2,1)} %get-tuple-element.11.colw_h, f32[8,128]{1,0:T(8,128)} %get-tuple-element.12.cover_h, ...), custom_call_target="tpu_custom_call" | custom-call | tf_op jit(solution)/shard_map/tiles/pallas_call | solution.py:810

commit v3 on v2

--- a/solution.py
+++ b/solution.py
@@ -27,7 +27,7 @@
 FIRST_MAX = 64 - WIN
 FAR = 1000.0
 FAR_STEPS = 4
-TILE_VMEM = 60 * 1024 * 1024
+TILE_VMEM = 14 * 1024 * 1024
 
 
 def iota(shape, dim):
@@ -426,8 +426,9 @@
             valid = (chosen >= 0) & (chosen < 32)
             granule = jnp.where(valid, chosen % 16, 0)
             first = [jnp.clip(pick // SP - 1, 0, FIRST_MAX) for pick in picks]
-            for column, value in enumerate((granule, first[0] // 2, first[1])):
-                table = jnp.where(lane == rank * 3 + column, value, table)
+            turns = [(b * 16 + 128 - first[1]) % 128 for b in range(BD_)]
+            for column, value in enumerate((granule, (first[0] // 2) * 2, *turns)):
+                table = jnp.where(lane == rank * 5 + column, value, table)
         tab_v[...] = table
         copy = pltpu.make_async_copy(tab_v, tab_s, tab_sem)
         copy.start()
@@ -545,15 +546,14 @@
 
     def fill(t):
         for rank in range(2):
-            granule = tab_s[t, rank * 3]
-            row = tab_s[t, rank * 3 + 1]
-            column = tab_s[t, rank * 3 + 2]
+            granule = tab_s[t, rank * 5]
+            row = tab_s[t, rank * 5 + 1]
             halves = []
             for c in range(2):
                 value = None
                 for b in range(BD_):
-                    x = out_b[granule, b, pl.ds(2 * row + c, 8, stride=2), :]
-                    x = pltpu.roll(x, lax.rem(b * 16 + 128 - column, 128), axis=1)
+                    x = out_b[granule, b, pl.ds(row + c, 8, stride=2), :]
+                    x = pltpu.roll(x, tab_s[t, rank * 5 + 2 + b], axis=1)
                     value = x if value is None else jnp.where(lane_band == b, x, value)
                 halves.append(value)
             pay_out[t, rank * 16 : rank * 16 + 16, :] = jnp.concatenate(halves, axis=0).astype(BF16)
@@ -584,6 +584,15 @@
     own_copy = pltpu.make_async_copy(pay_out.at[me], pay_in.at[me], own_sem)
     own_copy.start()
     own_copy.wait()
+    for sweep in range(SWEEPS):
+        for side in range(2):
+            for piece in range(REACH + 1):
+                halo_copy(sweep, side, piece).wait_send()
+        for part in range(3):
+            for k in range(1, NB):
+                part_copy(sweep, part, k).wait_send()
+    for save in saves:
+        save.wait()
 
     def take_pay(k, carry):
         pltpu.make_async_remote_copy(
@@ -598,21 +607,11 @@
 
     lax.fori_loop(1, NG, take_pay, 0)
 
-    for sweep in range(SWEEPS):
-        for side in range(2):
-            for piece in range(REACH + 1):
-                halo_copy(sweep, side, piece).wait_send()
-        for part in range(3):
-            for k in range(1, NB):
-                part_copy(sweep, part, k).wait_send()
-
     def sent_pay(k, carry):
         pay_copy(k).wait_send()
         return carry
 
     lax.fori_loop(1, NG, sent_pay, 0)
-    for save in saves:
-        save.wait()
 
 
 def tile_kernel(
@@ -662,28 +661,25 @@
     lane8 = iota((8, 128), 1)
     loads[0].wait()
 
-    def expand(group, carry):
-        rank = group // 2
-        base = lax.rem(group, 2) * 16
-        for s in range(16):
-            block = pay_in[base + s, pl.ds(pl.multiple_of(rank * 16, 16), 16), :].astype(F32)
-            for c in range(2):
-                x = block[c * 8 : c * 8 + 8]
-                for b in range(BD_):
+    def expand(b):
+        for group in range(4):
+            rank, base = group // 2, (group % 2) * 16
+            for s in range(16):
+                block = pay_in[base + s, rank * 16 : rank * 16 + 16, :].astype(F32)
+                for c in range(2):
                     parts = []
                     for parity in range(2):
                         turn = ((s % 8) * 16 - parity * 64 - b * 16) % 128
-                        y = pltpu.roll(x, turn, axis=1) if turn else x
+                        y = block[c * 8 : c * 8 + 8]
+                        y = pltpu.roll(y, turn, axis=1) if turn else y
                         parts.append(jnp.where(lane8 // 16 == s % 8, y, 0.0))
                     diagonal[
                         group * 6 + b * 2 + c,
                         s * 16 : s * 16 + 16,
                         (s // 8) * 128 : (s // 8) * 128 + 128,
                     ] = jnp.concatenate(parts, axis=0).astype(BF16)
-        return carry
-
-    lax.fori_loop(0, 4, expand, 0)
-
+
+    expand(0)
     for load in loads[1:4]:
         load.wait()
     for load, save in zip(loads[5:], saves):
@@ -692,7 +688,9 @@
     loads[4].wait()
     inverse_cover = cover[0:1, 0:1]
 
-    def correct(b, carry):
+    for b in range(BD_):
+        if b + 1 < BD_:
+            expand(b + 1)
         fields = []
         for c in range(2):
             for group in range(4):
@@ -703,9 +701,7 @@
         value = pixels * (1.0 + fields[0] * inverse_cover) + fields[1] * inverse_cover
         tile_b[b] = value.astype(BF16)
         pltpu.make_async_copy(tile_b.at[b], tile_h.at[b], out_sem.at[4 + b]).start()
-        return carry
-
-    lax.fori_loop(0, BD_, correct, 0)
+
     for save in saves:
         save.wait()
     for b in range(BD_):
@@ -739,6 +735,7 @@
         .reshape(GD, BD_, 256, 128)
     )
     any_ = pl.BlockSpec(memory_space=pl.ANY)
+    hbm = pl.BlockSpec(memory_space=pltpu.HBM)
     dma = pltpu.SemaphoreType.DMA
     middle, payload, roww, colw, cover = pl.pallas_call(
         kernel,
@@ -749,7 +746,7 @@
             jax.ShapeDtypeStruct((1024, PIX), BF16),
             jax.ShapeDtypeStruct((8, 128), F32),
         ),
-        in_specs=[any_] * 9,
+        in_specs=[hbm] * 9,
         out_specs=(any_,) * 5,
         scratch_shapes=[
             pltpu.SMEM((SLOTS, GD), I32),
@@ -793,19 +790,24 @@
             pltpu.SemaphoreType.REGULAR((FAR_STEPS, 2)),
         ],
         compiler_params=pltpu.CompilerParams(
-            collective_id=0, has_side_effects=True, vmem_limit_bytes=60 * 1024 * 1024
+            collective_id=0, has_side_effects=True, vmem_limit_bytes=36 * 1024 * 1024
         ),
         name="balance",
     )(
-        neighbour_offset.T,
-        neighbour_count,
-        prior,
-        rhs,
-        diag,
-        cross,
-        coupling,
-        tile_route.T,
-        tile_window.transpose(1, 2, 0),
+        *(
+            pltpu.with_memory_space_constraint(x, pltpu.HBM)
+            for x in (
+                neighbour_offset.T,
+                neighbour_count,
+                prior,
+                rhs,
+                diag,
+                cross,
+                coupling,
+                tile_route.T,
+                tile_window.transpose(1, 2, 0),
+            )
+        )
     )
     balanced, tiles = pl.pallas_call(
         tile_kernel,

time: 48 us -> 46.9 us (0.977)
  Pallas kernels: 47.2 us -> 46.1 us
    pallas_call x1, Pallas kernels: 5.16 us -> 4.18 us  [per_device(): pl.pallas_call(tile_kernel, out_shape=(jax.ShapeDtypeStruct((GD, BD_, 64,...]
where the time goes in v3:
time: 46.9 us; the launch traced here: 46.8 us
  Pallas kernels  46.1 us (98%)
  between operations  0.66 us (1%)
    pallas_call x1, Pallas kernels, per_device(): pl.pallas_call(kernel, out_shape=(jax.ShapeDtypeStruct((GD, BD_, 64, 128)...  41.9 us
    pallas_call x1, Pallas kernels, per_device(): pl.pallas_call(tile_kernel, out_shape=(jax.ShapeDtypeStruct((GD, BD_, 64,...  4.18 us

profile of v3, /device:TPU:1, one launch (start us, length us, event | category | flops | bytes accessed | tf_op | source)
XLA Modules:
  0.0 46.8 jit_solution(6215308712195961226)
XLA Ops:
  0.6 0.0 copy-start
  0.6 41.9 %balance.1 = (f32[16,3,64,128]{3,2,1,0:T(8,128)S(1)}, bf16[32,32,128]{2,1,0:T(8,128)(2,1)S(1)}, bf16[256,1024]{1,0:T(8,128)(2,1)S(1)}, bf16[1024,256]{1,0:T(8,128)(2,1)S(1)}, f32[8,128]{1,0:T(8,128)S(1)}) custom-call(s32[8,16]{1,0:T(8,128)} %bitcast.42, s32[16]{0:T(128)} %cnt_h.1, f32[16,3,64,128]{3,2,1,0:T(8,128)} %bitcast.37, f32[16,3,64,128]{3,2,1,0:T(8,128)} %bitcast.38, ...), custom_call_target="tpu_custom_call" | custom-call | tf_op jit(solution)/shard_map/balance/pallas_call | solution.py:740
  42.6 0.0 copy-done
  42.6 4.2 %tiles.1 = (f32[16,3,64,128]{3,2,1,0:T(8,128)}, bf16[3,256,256]{2,1,0:T(8,128)(2,1)}) custom-call(bf16[32,32,128]{2,1,0:T(8,128)(2,1)S(1)} %get-tuple-element.9.pay_h, bf16[256,1024]{1,0:T(8,128)(2,1)S(1)} %get-tuple-element.10.roww_h, bf16[1024,256]{1,0:T(8,128)(2,1)S(1)} %get-tuple-element.11.colw_h, f32[8,128]{1,0:T(8,128)S(1)} %get-tuple-element.12.cover_h, ...), custom_call_target="tpu_custom_call" | custom-call | tf_op jit(solution)/shard_map/tiles/pallas_call | solution.py:812
Async XLA Ops:
  0.6 41.9 %copy-start = (bf16[1,3,256,256]{3,2,1,0:T(8,128)(2,1)S(1)}, bf16[1,3,256,256]{3,2,1,0:T(8,128)(2,1)}, u32[]{:S(2)}) copy-start(bf16[1,3,256,256]{3,2,1,0:T(8,128)(2,1)} %param.19) | copy-start | bytes 1179652

commit v4 on v3

--- a/solution.py
+++ b/solution.py
@@ -532,9 +532,8 @@
             take_cross()
             loads[8].wait()
         solve(0, sweep)
-        if sweep == 1:
+        if sweep == 2:
             send_table()
-        elif sweep == 2:
             far_wait(3)
         for part in order:
             take_grids(sweep, part - 1)

time: 46.9 us -> 47.8 us (1.019)
  Pallas kernels: 46.1 us -> 47 us
    pallas_call x1, Pallas kernels: 41.9 us -> 42.8 us  [per_device(): pl.pallas_call(kernel, out_shape=(jax.ShapeDtypeStruct((GD, BD_, 64, 128)...]
where the time goes in v4:
time: 47.8 us; the launch traced here: 47.6 us
  Pallas kernels  47 us (98%)
  between operations  0.66 us (1%)
    pallas_call x1, Pallas kernels, per_device(): pl.pallas_call(kernel, out_shape=(jax.ShapeDtypeStruct((GD, BD_, 64, 128)...  42.8 us
    pallas_call x1, Pallas kernels, per_device(): pl.pallas_call(tile_kernel, out_shape=(jax.ShapeDtypeStruct((GD, BD_, 64,...  4.18 us

profile of v4, /device:TPU:1, one launch (start us, length us, event | category | flops | bytes accessed | tf_op | source)
XLA Modules:
  0.0 47.6 jit_solution(12986934904216538057)
XLA Ops:
  0.6 0.0 copy-start
  0.6 42.8 %balance.1 = (f32[16,3,64,128]{3,2,1,0:T(8,128)S(1)}, bf16[32,32,128]{2,1,0:T(8,128)(2,1)S(1)}, bf16[256,1024]{1,0:T(8,128)(2,1)S(1)}, bf16[1024,256]{1,0:T(8,128)(2,1)S(1)}, f32[8,128]{1,0:T(8,128)S(1)}) custom-call(s32[8,16]{1,0:T(8,128)} %bitcast.42, s32[16]{0:T(128)} %cnt_h.1, f32[16,3,64,128]{3,2,1,0:T(8,128)} %bitcast.37, f32[16,3,64,128]{3,2,1,0:T(8,128)} %bitcast.38, ...), custom_call_target="tpu_custom_call" | custom-call | tf_op jit(solution)/shard_map/balance/pallas_call | solution.py:739
  43.4 0.0 copy-done
  43.4 4.2 %tiles.1 = (f32[16,3,64,128]{3,2,1,0:T(8,128)}, bf16[3,256,256]{2,1,0:T(8,128)(2,1)}) custom-call(bf16[32,32,128]{2,1,0:T(8,128)(2,1)S(1)} %get-tuple-element.9.pay_h, bf16[256,1024]{1,0:T(8,128)(2,1)S(1)} %get-tuple-element.10.roww_h, bf16[1024,256]{1,0:T(8,128)(2,1)S(1)} %get-tuple-element.11.colw_h, f32[8,128]{1,0:T(8,128)S(1)} %get-tuple-element.12.cover_h, ...), custom_call_target="tpu_custom_call" | custom-call | tf_op jit(solution)/shard_map/tiles/pallas_call | solution.py:811
Async XLA Ops:
  0.6 42.8 %copy-start = (bf16[1,3,256,256]{3,2,1,0:T(8,128)(2,1)S(1)}, bf16[1,3,256,256]{3,2,1,0:T(8,128)(2,1)}, u32[]{:S(2)}) copy-start(bf16[1,3,256,256]{3,2,1,0:T(8,128)(2,1)} %param.19) | copy-start | bytes 1179652

commit v5 on v3

--- a/solution.py
+++ b/solution.py
@@ -430,9 +430,7 @@
             for column, value in enumerate((granule, (first[0] // 2) * 2, *turns)):
                 table = jnp.where(lane == rank * 5 + column, value, table)
         tab_v[...] = table
-        copy = pltpu.make_async_copy(tab_v, tab_s, tab_sem)
-        copy.start()
-        copy.wait()
+        pltpu.make_async_copy(tab_v, tab_s, tab_sem).start()
 
     def weights(coord, ref):
         lane = iota((8, 512), 1)
@@ -580,6 +578,7 @@
 
         return carry
 
+    pltpu.make_async_copy(tab_v, tab_s, tab_sem).wait()
     lax.fori_loop(0, NG // 4, fill_and_send, 0)
     own_copy = pltpu.make_async_copy(pay_out.at[me], pay_in.at[me], own_sem)
     own_copy.start()

time: 46.9 us -> 46.5 us (level)
  no operation moved by 1% of the time
where the time goes in v5:
time: 46.5 us; the launch traced here: 46.4 us
  Pallas kernels  45.7 us (98%)
  between operations  0.66 us (1%)
    pallas_call x1, Pallas kernels, per_device(): pl.pallas_call(kernel, out_shape=(jax.ShapeDtypeStruct((GD, BD_, 64, 128)...  41.6 us
    pallas_call x1, Pallas kernels, per_device(): pl.pallas_call(tile_kernel, out_shape=(jax.ShapeDtypeStruct((GD, BD_, 64,...  4.18 us

profile of v5, /device:TPU:1, one launch (start us, length us, event | category | flops | bytes accessed | tf_op | source)
XLA Modules:
  0.0 46.4 jit_solution(15455346173100919152)
XLA Ops:
  0.6 0.0 copy-start
  0.6 41.6 %balance.1 = (f32[16,3,64,128]{3,2,1,0:T(8,128)S(1)}, bf16[32,32,128]{2,1,0:T(8,128)(2,1)S(1)}, bf16[256,1024]{1,0:T(8,128)(2,1)S(1)}, bf16[1024,256]{1,0:T(8,128)(2,1)S(1)}, f32[8,128]{1,0:T(8,128)S(1)}) custom-call(s32[8,16]{1,0:T(8,128)} %bitcast.42, s32[16]{0:T(128)} %cnt_h.1, f32[16,3,64,128]{3,2,1,0:T(8,128)} %bitcast.37, f32[16,3,64,128]{3,2,1,0:T(8,128)} %bitcast.38, ...), custom_call_target="tpu_custom_call" | custom-call | tf_op jit(solution)/shard_map/balance/pallas_call | solution.py:739
  42.2 0.0 copy-done
  42.2 4.2 %tiles.1 = (f32[16,3,64,128]{3,2,1,0:T(8,128)}, bf16[3,256,256]{2,1,0:T(8,128)(2,1)}) custom-call(bf16[32,32,128]{2,1,0:T(8,128)(2,1)S(1)} %get-tuple-element.9.pay_h, bf16[256,1024]{1,0:T(8,128)(2,1)S(1)} %get-tuple-element.10.roww_h, bf16[1024,256]{1,0:T(8,128)(2,1)S(1)} %get-tuple-element.11.colw_h, f32[8,128]{1,0:T(8,128)S(1)} %get-tuple-element.12.cover_h, ...), custom_call_target="tpu_custom_call" | custom-call | tf_op jit(solution)/shard_map/tiles/pallas_call | solution.py:811
Async XLA Ops:
  0.6 41.6 %copy-start = (bf16[1,3,256,256]{3,2,1,0:T(8,128)(2,1)S(1)}, bf16[1,3,256,256]{3,2,1,0:T(8,128)(2,1)}, u32[]{:S(2)}) copy-start(bf16[1,3,256,256]{3,2,1,0:T(8,128)(2,1)} %param.19) | copy-start | bytes 1179652
